TPU v7x, 32 devices: a whole 2x2x4 slice. The times are simulated.
32 devices in a mesh: seq: 8 (over z, x), head: 4 (over y, core).
Axes of the slice: x: 2, y: 2, z: 4, core: 2. Of those that a mesh axis runs over, the one named last changes fastest.
Arguments:
- features: bfloat16 [8192, 8192], P(('seq', 'head')), may hold values from -6 to 6
- gate_input: bfloat16 [8192, 8192], P(('seq', 'head')), may hold values from -6 to 6
- bmat: bfloat16 [8192, 8, 128], P(('seq', 'head')), may hold values from -1.78125 to 1.78125
- cmat: bfloat16 [8192, 8, 128], P(('seq', 'head')), may hold values from -1.78125 to 1.78125
- step_size: float32 [8192, 128], P(('seq', 'head')), may hold values from 0.001 to 0.1
- log_decay: float32 [8192, 128], P(('seq', 'head')), may hold values from -0.8 to 0
- skip: float32 [128], P('head'), may hold values from 0.5 to 2
- norm_gain: float32 [8192], replicated, may hold values from 0.1 to 1.9
Outputs:
- mixed: bfloat16 [8192, 8192], P(('seq', 'head'))
All inputs are finite; a program needn't handle non-finite values.
Results may differ from a plain program's by a relative error of at most 0.0085.
Values may be sent and summed in bfloat16 or wider, within the bound.
No kernel may reach another device: no remote copies, remote signals or barrier semaphores. Data moves between devices by JAX's collectives and lax.ppermute only.
A program may use at most 128 MiB of HBM per device.

v0:
```python
import jax
import jax.numpy as jnp
from jax import lax
from jax.sharding import PartitionSpec as P

SPAN = 256


def passed_along(value, axis, steps):
    count = lax.axis_size(axis)
    leading, last = (max(0, -steps), min(count, count - steps))
    return lax.ppermute(value, axis, [(source, source + steps) for source in range(leading, last)])


def block_terms(feature_block, b_block, c_block, dt_block, cum_block):
    length = cum_block.shape[0]
    token_positions = jnp.arange(length)
    causal = token_positions[:, None] >= token_positions[None, :]
    scores = jnp.einsum("tgn,sgn->gts", c_block, b_block, preferred_element_type=jnp.float32)
    cum_heads = jnp.transpose(cum_block, (1, 2, 0))
    spread = cum_heads[:, :, :, None] - cum_heads[:, :, None, :]
    step_scale = jnp.transpose(dt_block, (1, 2, 0))[:, :, None, :]
    weights = jnp.where(
        causal, scores[:, None] * jnp.exp(jnp.where(causal, spread, 0.0)) * step_scale, 0.0
    ).astype(jnp.bfloat16)
    intra_terms = jnp.einsum(
        "ghts,sghp->tghp", weights, feature_block, preferred_element_type=jnp.float32
    )
    tail_scale = jnp.exp(cum_block[-1:] - cum_block) * dt_block
    loaded = (b_block[:, :, None, :].astype(jnp.float32) * tail_scale[..., None]).astype(
        jnp.bfloat16
    )
    update = jnp.einsum(
        "sghn,sghp->ghpn", loaded, feature_block, preferred_element_type=jnp.float32
    )
    return (intra_terms, update)


def normalize(values, gate_part, gain_row):
    gated_values = values.astype(jnp.float32) * jax.nn.silu(gate_part.astype(jnp.float32))
    inverse_rms = lax.rsqrt(jnp.mean(gated_values * gated_values, axis=-1, keepdims=True) + 1e-05)
    return (gated_values * inverse_rms * gain_row).astype(jnp.bfloat16)


def pair_terms(members):
    return jax.vmap(block_terms)(*members)


def shards(features, gate_input, bmat, cmat, step_size, log_decay, skip, norm_gain):
    tok_rows = features.shape[0]
    group_count = bmat.shape[1]
    state_size = bmat.shape[2]
    heads_total = step_size.shape[1]
    per_group = heads_total // group_count
    group_width = features.shape[1] // group_count
    head_size = group_width // per_group
    feature_groups = features.reshape(tok_rows, group_count, group_width)
    gate_groups = gate_input.reshape(tok_rows, group_count, group_width)
    dt_groups = step_size.reshape(tok_rows, group_count, per_group)
    decay_groups = log_decay.reshape(tok_rows, group_count, per_group)
    feature_here, gate_here, b_here, c_here = (
        lax.all_to_all(feature_groups, "head", split_axis=1, concat_axis=0, tiled=True),
        lax.all_to_all(gate_groups, "head", split_axis=1, concat_axis=0, tiled=True),
        lax.all_to_all(bmat, "head", split_axis=1, concat_axis=0, tiled=True),
        lax.all_to_all(cmat, "head", split_axis=1, concat_axis=0, tiled=True),
    )
    dt_here, decay_here = (
        lax.all_to_all(dt_groups, "head", split_axis=1, concat_axis=0, tiled=True),
        lax.all_to_all(decay_groups, "head", split_axis=1, concat_axis=0, tiled=True),
    )
    seq_rows = feature_here.shape[0]
    local_groups = feature_here.shape[1]
    blocks = seq_rows // SPAN
    feature_blocks = feature_here.reshape(blocks, SPAN, local_groups, per_group, head_size)
    b_blocks = b_here.reshape(blocks, SPAN, local_groups, state_size)
    c_blocks = c_here.reshape(blocks, SPAN, local_groups, state_size)
    dt_blocks = dt_here.reshape(blocks, SPAN, local_groups, per_group)
    decay_blocks = decay_here.reshape(blocks, SPAN, local_groups, per_group)
    cum_blocks = jnp.cumsum(decay_blocks, axis=1)

    def paired(array):
        return array.reshape((blocks // 2, 2) + array.shape[1:])

    intra_terms, updates = lax.map(
        pair_terms,
        (
            paired(feature_blocks),
            paired(b_blocks),
            paired(c_blocks),
            paired(dt_blocks),
            paired(cum_blocks),
        ),
    )
    intra_terms = intra_terms.reshape(blocks, SPAN, local_groups, per_group, head_size)
    updates = updates.reshape(blocks, local_groups, per_group, head_size, state_size)
    block_decay = jnp.exp(cum_blocks[:, -1])

    def advance(carry_state, members):
        decay_now, update_now = members
        return (decay_now[..., None, None] * carry_state + update_now, carry_state)

    start_state = jnp.zeros((local_groups, per_group, head_size, state_size), jnp.float32)
    local_end, local_states = lax.scan(advance, start_state, (block_decay, updates))
    block_sums = jnp.sum(decay_blocks, axis=1)
    before = jnp.cumsum(block_sums, axis=0) - block_sums
    shard_decay = jnp.exp(jnp.sum(block_sums, axis=0))

    def hop(iteration, incoming):
        return passed_along(shard_decay[..., None, None] * incoming + local_end, "seq", 1)

    entering = lax.fori_loop(0, lax.axis_size("seq") - 1, hop, jnp.zeros_like(local_end))
    states = local_states + jnp.exp(before)[..., None, None] * entering[None]
    carried = (
        jnp.einsum(
            "ktgn,kghpn->ktghp",
            c_blocks.astype(jnp.float32),
            states,
            precision=lax.Precision.HIGHEST,
        )
        * jnp.exp(cum_blocks)[..., None]
    )
    head_skip = skip.reshape(local_groups, per_group)
    ssm_out = (
        intra_terms
        + carried
        + head_skip[None, None, :, :, None] * feature_blocks.astype(jnp.float32)
    ).astype(jnp.bfloat16)
    ssm_out = ssm_out.reshape(seq_rows, local_groups, group_width)
    offset = lax.axis_index("head") * (local_groups * group_width)
    gain_here = lax.dynamic_slice_in_dim(norm_gain, offset, local_groups * group_width).reshape(
        local_groups, group_width
    )
    mixed_here = normalize(ssm_out, gate_here, gain_here)
    restored = lax.all_to_all(mixed_here, "head", split_axis=0, concat_axis=1, tiled=True)
    return restored.reshape(tok_rows, features.shape[1])


def solution(mesh):
    return jax.shard_map(
        shards,
        mesh=mesh,
        in_specs=(
            P(("seq", "head"), None),
            P(("seq", "head"), None),
            P(("seq", "head"), None, None),
            P(("seq", "head"), None, None),
            P(("seq", "head"), None),
            P(("seq", "head"), None),
            P("head"),
            P(),
        ),
        out_specs=P(("seq", "head"), None),
        check_vma=False,
    )
```

profile of v0, /device:TPU:8, one launch (start us, length us, event | category | flops | bytes accessed | tf_op | source)
XLA Modules:
  0.0 477.8 jit_solution(16098080593060179614)
XLA Ops:
  21.6 6.4 %copy.118 = bf16[256,8192]{0,1:T(8,128)(2,1)} copy(bf16[256,8192]{1,0:T(8,128)(2,1)} %param.14) | data formatting | bytes 8388608 | tf_op args[0]
  28.0 6.5 %copy.119 = bf16[256,8,1024]{2,0,1:T(8,128)(2,1)} copy(bf16[256,8,1024]{0,2,1:T(8,128)(2,1)} %bitcast.164) | data formatting | bytes 8388608 | tf_op jit(solution)/shard_map/reshape | solution.py:57
  40.4 6.4 %copy.132 = bf16[256,8192]{0,1:T(8,128)(2,1)} copy(bf16[256,8192]{1,0:T(8,128)(2,1)} %param.15) | data formatting | bytes 8388608 | tf_op args[1]
  53.3 34.5 %all-to-all-done = bf16[256,8,1024]{2,0,1:T(8,128)(2,1)} async-done(((bf16[256,8,1024]{2,0,1:T(8,128)(2,1)}), bf16[256,8,1024]{2,0,1:T(8,128)(2,1)}, u32[]{:S(2)}, u32[]{:S(2)}) %all-to-all-start) | async-done | bytes 4194336 | tf_op jit(solution)/shard_map/all_to_all | solution.py:62
  91.5 6.2 %copy.120 = bf16[256,4,2,1024]{0,3,2,1:T(8,128)(2,1)} copy(bf16[256,4,2,1024]{3,0,2,1:T(8,128)(2,1)} %bitcast.13) | data formatting | bytes 8388608 | tf_op jit(solution)/shard_map/all_to_all | solution.py:62
  100.0 5.0 %all-to-all-start.5 = ((bf16[256,8,1024]{0,2,1:T(8,128)(2,1)}), bf16[256,8,1024]{0,2,1:T(8,128)(2,1)}, u32[]{:S(2)}, u32[]{:S(2)}) async-start(bf16[256,8,1024]{0,2,1:T(8,128)(2,1)} %bitcast.161), calls=%async_computation.5 | async-start | bytes 8388608 | tf_op jit(solution)/shard_map/all_to_all | solution.py:63
  105.0 31.4 %while.35 = (s32[]{:T(128)}, f32[2,2,256,2,16,64]{2,5,4,3,1,0:T(8,128)}, f32[2,2,2,16,64,128]{5,4,3,2,1,0:T(8,128)}, bf16[2,2,256,2,16,64]{2,5,4,3,1,0:T(8,128)(...) while((s32[]{:T(128)}, ...), condition=%wide.region_3.4_spmd, body=%wide.region_2.3_spmd.sunk | while | flops 902004736 | bytes 15929189 | solution.py:84
  107.6 7.3 %bitcast_dynamic-update-slice_fusion.6 = f32[2,2,256,2,16,64]{2,5,4,3,1,0:T(8,128)} fusion(f32[2,2,256,2,16,64]{2,5,4,3,1,0:T(8,128)} %get-tuple-element.328, s32[]{:T(128)} %get-tuple-element.327, f32[2,2,16,256]{3,2,1,0:T(8,128)S(1)} %copy.162, f32[2,2,16,256]{3,2,1,0:T(8,128)S(1)} %copy.164, f32[2,2,256,256]{3,2,1,0:T(8,128)S(1)} %fusion.52, ...), kind=kOutput, calls=%fused_computation.10.clone.1 | convolution fusion | flops 562036736 | bytes 7603200 | tf_op jit(solution)/shard_map/while/body/eval_jaxpr/vmap(ghts,sghp->tghp)/dot_general | solution.py:26
  115.6 5.1 %bitcast_dynamic-update-slice_fusion.7 = f32[2,2,2,16,64,128]{5,4,3,2,1,0:T(8,128)} fusion(f32[2,2,2,16,64,128]{5,4,3,2,1,0:T(8,128)} %get-tuple-element.329, s32[]{:T(128)} %get-tuple-element.327, f32[2,256,2,16]{1,3,2,0:T(8,128)S(1)} %copy.165, f32[2,256,2,128]{3,1,2,0:T(8,128)S(1)} %bitcast_convert_fusion.2, ...), kind=kOutput, calls=%fused_computation.13.clone.1 | convolution fusion | flops 272629760 | bytes 4785152 | tf_op jit(solution)/shard_map/while/body/eval_jaxpr/vmap(sghn,sghp->ghpn)/dot_general | solution.py:33
  123.3 7.3 %bitcast_dynamic-update-slice_fusion.6 = f32[2,2,256,2,16,64]{2,5,4,3,1,0:T(8,128)} fusion(f32[2,2,256,2,16,64]{2,5,4,3,1,0:T(8,128)} %get-tuple-element.328, s32[]{:T(128)} %get-tuple-element.327, f32[2,2,16,256]{3,2,1,0:T(8,128)S(1)} %copy.162, f32[2,2,16,256]{3,2,1,0:T(8,128)S(1)} %copy.164, f32[2,2,256,256]{3,2,1,0:T(8,128)S(1)} %fusion.52, ...), kind=kOutput, calls=%fused_computation.10.clone.1 | convolution fusion | flops 562036736 | bytes 7603200 | tf_op jit(solution)/shard_map/while/body/eval_jaxpr/vmap(ghts,sghp->tghp)/dot_general | solution.py:26
  131.3 5.1 %bitcast_dynamic-update-slice_fusion.7 = f32[2,2,2,16,64,128]{5,4,3,2,1,0:T(8,128)} fusion(f32[2,2,2,16,64,128]{5,4,3,2,1,0:T(8,128)} %get-tuple-element.329, s32[]{:T(128)} %get-tuple-element.327, f32[2,256,2,16]{1,3,2,0:T(8,128)S(1)} %copy.165, f32[2,256,2,128]{3,1,2,0:T(8,128)S(1)} %bitcast_convert_fusion.2, ...), kind=kOutput, calls=%fused_computation.13.clone.1 | convolution fusion | flops 272629760 | bytes 4785152 | tf_op jit(solution)/shard_map/while/body/eval_jaxpr/vmap(sghn,sghp->ghpn)/dot_general | solution.py:33
  136.5 10.0 %while.37 = (s32[]{:T(128)}, f32[2,16,64,128]{3,2,1,0:T(8,128)S(1)}, f32[4,2,16,64,128]{4,3,2,1,0:T(8,128)}, f32[4,2,16]{2,1,0:T(2,128)S(1)}, f32[4,2,16,64,128]{4,3,2,1,0:T(8,128)}, /*index=5*/s32[]{:T(128)}, s32[]{:T(128)}) while((s32[]{:T(128)}, f32[2,16,64,128]{3,2,1,0:T(8,128)S(1)}, f32[4,2,16,64,128]{4,3,2,1,0:T(8,128)}, ...), condition=%wide.region_5.6_spmd.clone, body=%wide.region_4.5_spmd.clone.sunk | while | flops 1048579 | bytes 5243872 | solution.py:103
  146.5 6.6 %all-to-all-done.5 = bf16[256,8,1024]{0,2,1:T(8,128)(2,1)} async-done(((bf16[256,8,1024]{0,2,1:T(8,128)(2,1)}), bf16[256,8,1024]{0,2,1:T(8,128)(2,1)}, u32[]{:S(2)}, u32[]{:S(2)}) %all-to-all-start.5) | async-done | bytes 4194336 | tf_op jit(solution)/shard_map/all_to_all | solution.py:63
  153.0 6.2 %convert_element_type.75 = f32[256,8,1024]{0,2,1:T(8,128)} convert(bf16[256,8,1024]{0,2,1:T(8,128)(2,1)} %all-to-all-done.5) | non-fusion elementwise | flops 2097152 | bytes 12582912 | tf_op jit(solution)/shard_map/convert_element_type | solution.py:40
  159.3 175.0 %while.36 = (s32[]{:T(128)}, f32[2,16,64,128]{3,2,1,0:T(8,128)S(1)}, f32[2,16]{1,0:T(2,128)S(1)}, f32[2,16,64,128]{3,2,1,0:T(8,128)S(1)}, s32[]{:T(128)}) while((s32[]{:T(128)}, f32[2,16,64,128]{3,2,1,0:T(8,128)S(1)}, f32[2,16]{1,0:T(2,128)S(1)}, f32[2,16,64,128]{3,2,1,0:T(8,128)S(1)}, s32[]{:T(128)}) %tuple.65), condition=%wide.region_10.11_spmd, body=%wide.region_9.10_spmd.sunk | while | flops 524290 | bytes 7340261 | solution.py:111
  162.9 24.0 %collective-permute-done = f32[2,16,64,128]{3,2,1,0:T(8,128)S(1)} collective-permute-done((f32[2,16,64,128]{3,2,1,0:T(8,128)S(1)}, f32[2,16,64,128]{3,2,1,0:T(8,128)S(1)}, u32[]{:S(2)}, u32[]{:S(2)}) %collective-permute-start) | collective-permute-done | bytes 1048608 | tf_op jit(solution)/shard_map/while/body/eval_jaxpr/ppermute | solution.py:12
  189.6 24.0 %collective-permute-done = f32[2,16,64,128]{3,2,1,0:T(8,128)S(1)} collective-permute-done((f32[2,16,64,128]{3,2,1,0:T(8,128)S(1)}, f32[2,16,64,128]{3,2,1,0:T(8,128)S(1)}, u32[]{:S(2)}, u32[]{:S(2)}) %collective-permute-start) | collective-permute-done | bytes 1048608 | tf_op jit(solution)/shard_map/while/body/eval_jaxpr/ppermute | solution.py:12
  215.7 23.8 %collective-permute-done = f32[2,16,64,128]{3,2,1,0:T(8,128)S(1)} collective-permute-done((f32[2,16,64,128]{3,2,1,0:T(8,128)S(1)}, f32[2,16,64,128]{3,2,1,0:T(8,128)S(1)}, u32[]{:S(2)}, u32[]{:S(2)}) %collective-permute-start) | collective-permute-done | bytes 1048608 | tf_op jit(solution)/shard_map/while/body/eval_jaxpr/ppermute | solution.py:12
  241.6 22.9 %collective-permute-done = f32[2,16,64,128]{3,2,1,0:T(8,128)S(1)} collective-permute-done((f32[2,16,64,128]{3,2,1,0:T(8,128)S(1)}, f32[2,16,64,128]{3,2,1,0:T(8,128)S(1)}, u32[]{:S(2)}, u32[]{:S(2)}) %collective-permute-start) | collective-permute-done | bytes 1048608 | tf_op jit(solution)/shard_map/while/body/eval_jaxpr/ppermute | solution.py:12
  266.6 22.0 %collective-permute-done = f32[2,16,64,128]{3,2,1,0:T(8,128)S(1)} collective-permute-done((f32[2,16,64,128]{3,2,1,0:T(8,128)S(1)}, f32[2,16,64,128]{3,2,1,0:T(8,128)S(1)}, u32[]{:S(2)}, u32[]{:S(2)}) %collective-permute-start) | collective-permute-done | bytes 1048608 | tf_op jit(solution)/shard_map/while/body/eval_jaxpr/ppermute | solution.py:12
  290.7 21.2 %collective-permute-done = f32[2,16,64,128]{3,2,1,0:T(8,128)S(1)} collective-permute-done((f32[2,16,64,128]{3,2,1,0:T(8,128)S(1)}, f32[2,16,64,128]{3,2,1,0:T(8,128)S(1)}, u32[]{:S(2)}, u32[]{:S(2)}) %collective-permute-start) | collective-permute-done | bytes 1048608 | tf_op jit(solution)/shard_map/while/body/eval_jaxpr/ppermute | solution.py:12
  314.0 20.3 %collective-permute-done = f32[2,16,64,128]{3,2,1,0:T(8,128)S(1)} collective-permute-done((f32[2,16,64,128]{3,2,1,0:T(8,128)S(1)}, f32[2,16,64,128]{3,2,1,0:T(8,128)S(1)}, u32[]{:S(2)}, u32[]{:S(2)}) %collective-permute-start) | collective-permute-done | bytes 1048608 | tf_op jit(solution)/shard_map/while/body/eval_jaxpr/ppermute | solution.py:12
  334.4 13.8 %multiply_reduce_fusion = (f32[4,256,2]{1,2,0:T(2,128)S(1)}, f32[4,256,2,16,64]{1,4,3,2,0:T(8,128)}) fusion(f32[4,256,2,16,64]{1,4,3,2,0:T(8,128)} %bitcast.157, bf16[4,256,2,16,64]{1,4,3,2,0:T(8,128)(2,1)} %bitcast.167, f32[2,16]{1,0:T(2,128)S(1)} %mul.128, f32[4,256,2,16]{1,3,2,0:T(8,128)S(1)} %bitcast_exponential_fusion, ...), kind=kOutput, calls=%fused_computation.43 | convolution fusion | flops 3252680704 | bytes 35267200 | tf_op jit(solution)/shard_map/ktgn,kghpn->ktghp/dot_general | solution.py:114
  348.2 13.8 %copy.131 = f32[4,256,2,16,64]{1,0,4,3,2:T(4,128)} copy(f32[4,256,2,16,64]{1,4,3,2,0:T(8,128)} %get-tuple-element.208) | data formatting | bytes 16777216 | tf_op jit(solution)/shard_map/convert_element_type | solution.py:40
  361.9 10.7 %reshape.131 = f32[1024,2,1024]{0,2,1:T(8,128)} reshape(f32[4,256,2,16,64]{1,0,4,3,2:T(4,128)} %copy.131) | data formatting | bytes 16777216 | tf_op jit(solution)/shard_map/convert_element_type | solution.py:40
  372.7 8.8 %copy.134 = f32[4,256,2,1024]{3,1,0,2:T(8,128)} copy(f32[4,256,2,1024]{1,3,2,0:T(8,128)} %bitcast.158) | data formatting | bytes 16777216 | tf_op jit(solution)/shard_map/convert_element_type | solution.py:40
  381.4 8.7 %copy.136 = f32[1024,2,1024]{0,2,1:T(8,128)} copy(f32[1024,2,1024]{2,0,1:T(8,128)} %bitcast.159) | data formatting | bytes 16777216 | tf_op jit(solution)/shard_map/convert_element_type | solution.py:40
  390.1 8.6 %multiply_convert_fusion.4 = bf16[1024,2,1024]{0,2,1:T(8,128)(2,1)} fusion(f32[1024,2,1024]{0,2,1:T(8,128)} %reshape.131, f32[1024,2,1024]{0,2,1:T(8,128)} %copy.136, f32[2,1024]{1,0:T(2,128)S(1)} %copy-done.1, f32[1024,2]{0,1:T(2,128)S(1)} %bitcast.174), kind=kLoop, calls=%fused_computation.42 | loop fusion | flops 16777216 | bytes 20987904 | tf_op jit(solution)/shard_map/convert_element_type | solution.py:42
  398.7 11.3 %copy.138 = bf16[1024,2,1024]{2,1,0:T(2,128)(2,1)} copy(bf16[1024,2,1024]{0,2,1:T(8,128)(2,1)} %multiply_convert_fusion.4) | data formatting | bytes 8388608 | tf_op jit(solution)/shard_map/convert_element_type | solution.py:42
  410.0 51.9 %all_to_all.96 = bf16[1024,2,1024]{2,1,0:T(2,128)(2,1)S(1)} all-to-all(bf16[1024,2,1024]{2,1,0:T(2,128)(2,1)} %copy.138), channel_id=1, replica_groups=mesh['seq'=8,'head'=4] {'head'}, dimensions={0} | all-to-all | bytes 8388608 | tf_op jit(solution)/shard_map/all_to_all | solution.py:134
  465.2 6.2 %copy.140 = bf16[256,4,2,1024]{0,3,2,1:T(8,128)(2,1)} copy(bf16[256,4,2,1024]{3,0,1,2:T(8,128)(2,1)} %bitcast.162) | data formatting | bytes 8388608 | tf_op jit(solution)/shard_map/all_to_all | solution.py:134
  471.5 6.3 %copy.141 = bf16[256,8192]{1,0:T(8,128)(2,1)} copy(bf16[256,8192]{0,1:T(8,128)(2,1)} %bitcast.163) | data formatting | bytes 8388608 | tf_op jit(solution)/shard_map/reshape | solution.py:135
  (91 shorter events, 76.2 us)
Async XLA Ops:
  1.7 7.9 %all-to-all-start.3 = ((f32[256,8,16]{0,2,1:T(8,128)}), f32[256,8,16]{0,2,1:T(8,128)S(1)}, u32[]{:S(2)}, u32[]{:S(2)}) async-start(f32[256,8,16]{0,2,1:T(8,128)} %bitcast.22), calls=%async_computation.3 | async-start | bytes 262144 | tf_op jit(solution)/shard_map/all_to_all | solution.py:69
  9.6 7.9 %all-to-all-start.4 = ((f32[256,8,16]{0,2,1:T(8,128)}), f32[256,8,16]{0,2,1:T(8,128)S(1)}, u32[]{:S(2)}, u32[]{:S(2)}) async-start(f32[256,8,16]{0,2,1:T(8,128)} %bitcast.28), calls=%async_computation.4 | async-start | bytes 262144 | tf_op jit(solution)/shard_map/all_to_all | solution.py:68
  17.5 17.1 %all-to-all-start.1 = ((bf16[256,8,128]{2,0,1:T(8,128)(2,1)}), bf16[256,8,128]{2,0,1:T(8,128)(2,1)}, u32[]{:S(2)}, u32[]{:S(2)}) async-start(bf16[256,8,128]{2,0,1:T(8,128)(2,1)} %copy.121), calls=%async_computation.1 | async-start | bytes 1048576 | tf_op jit(solution)/shard_map/all_to_all | solution.py:65
  28.0 11.6 %copy-start = (bf16[256,8,128]{2,1,0:T(8,128)(2,1)S(1)}, bf16[256,8,128]{2,1,0:T(8,128)(2,1)}, u32[]{:S(2)}) copy-start(bf16[256,8,128]{2,1,0:T(8,128)(2,1)} %param.16) | copy-start | bytes 1572868
  34.5 12.3 %copy-start.2 = (f32[32]{0:T(128)S(1)}, f32[32]{0:T(128)}, u32[]{:S(2)}) copy-start(f32[32]{0:T(128)} %param.20) | copy-start | bytes 388
  34.5 53.2 %all-to-all-start = ((bf16[256,8,1024]{2,0,1:T(8,128)(2,1)}), bf16[256,8,1024]{2,0,1:T(8,128)(2,1)}, u32[]{:S(2)}, u32[]{:S(2)}) async-start(bf16[256,8,1024]{2,0,1:T(8,128)(2,1)} %copy.119), calls=%async_computation | async-start | bytes 8388608 | tf_op jit(solution)/shard_map/all_to_all | solution.py:62
  87.7 12.3 %all-to-all-start.2 = ((bf16[256,8,128]{2,0,1:T(8,128)(2,1)}), bf16[256,8,128]{2,0,1:T(8,128)(2,1)S(1)}, u32[]{:S(2)}, u32[]{:S(2)}) async-start(bf16[256,8,128]{2,0,1:T(8,128)(2,1)} %copy.122), calls=%async_computation.2 | async-start | bytes 1048576 | tf_op jit(solution)/shard_map/all_to_all | solution.py:64
  100.0 53.1 %all-to-all-start.5 = ((bf16[256,8,1024]{0,2,1:T(8,128)(2,1)}), bf16[256,8,1024]{0,2,1:T(8,128)(2,1)}, u32[]{:S(2)}, u32[]{:S(2)}) async-start(bf16[256,8,1024]{0,2,1:T(8,128)(2,1)} %bitcast.161), calls=%async_computation.5 | async-start | bytes 8388608 | tf_op jit(solution)/shard_map/all_to_all | solution.py:63
  159.5 27.4 %collective-permute-start = (f32[2,16,64,128]{3,2,1,0:T(8,128)S(1)}, f32[2,16,64,128]{3,2,1,0:T(8,128)S(1)}, u32[]{:S(2)}, u32[]{:S(2)}) collective-permute-start(f32[2,16,64,128]{3,2,1,0:T(8,128)S(1)} %multiply_add_fusion.2), channel_id=1, source_target_pairs={{0,4},{4,8},{8,12},{12,16},{16,20},{20,24},{24,28},{1,5},{5,9},{9,... | collective-permute-start | bytes 3145736 | tf_op jit(solution)/shard_map/while/body/eval_jaxpr/ppermute | solution.py:12
  187.1 26.5 %collective-permute-start = (f32[2,16,64,128]{3,2,1,0:T(8,128)S(1)}, f32[2,16,64,128]{3,2,1,0:T(8,128)S(1)}, u32[]{:S(2)}, u32[]{:S(2)}) collective-permute-start(f32[2,16,64,128]{3,2,1,0:T(8,128)S(1)} %multiply_add_fusion.2), channel_id=1, source_target_pairs={{0,4},{4,8},{8,12},{12,16},{16,20},{20,24},{24,28},{1,5},{5,9},{9,... | collective-permute-start | bytes 3145736 | tf_op jit(solution)/shard_map/while/body/eval_jaxpr/ppermute | solution.py:12
  213.8 25.7 %collective-permute-start = (f32[2,16,64,128]{3,2,1,0:T(8,128)S(1)}, f32[2,16,64,128]{3,2,1,0:T(8,128)S(1)}, u32[]{:S(2)}, u32[]{:S(2)}) collective-permute-start(f32[2,16,64,128]{3,2,1,0:T(8,128)S(1)} %multiply_add_fusion.2), channel_id=1, source_target_pairs={{0,4},{4,8},{8,12},{12,16},{16,20},{20,24},{24,28},{1,5},{5,9},{9,... | collective-permute-start | bytes 3145736 | tf_op jit(solution)/shard_map/while/body/eval_jaxpr/ppermute | solution.py:12
  239.6 24.8 %collective-permute-start = (f32[2,16,64,128]{3,2,1,0:T(8,128)S(1)}, f32[2,16,64,128]{3,2,1,0:T(8,128)S(1)}, u32[]{:S(2)}, u32[]{:S(2)}) collective-permute-start(f32[2,16,64,128]{3,2,1,0:T(8,128)S(1)} %multiply_add_fusion.2), channel_id=1, source_target_pairs={{0,4},{4,8},{8,12},{12,16},{16,20},{20,24},{24,28},{1,5},{5,9},{9,... | collective-permute-start | bytes 3145736 | tf_op jit(solution)/shard_map/while/body/eval_jaxpr/ppermute | solution.py:12
  264.6 24.0 %collective-permute-start = (f32[2,16,64,128]{3,2,1,0:T(8,128)S(1)}, f32[2,16,64,128]{3,2,1,0:T(8,128)S(1)}, u32[]{:S(2)}, u32[]{:S(2)}) collective-permute-start(f32[2,16,64,128]{3,2,1,0:T(8,128)S(1)} %multiply_add_fusion.2), channel_id=1, source_target_pairs={{0,4},{4,8},{8,12},{12,16},{16,20},{20,24},{24,28},{1,5},{5,9},{9,... | collective-permute-start | bytes 3145736 | tf_op jit(solution)/shard_map/while/body/eval_jaxpr/ppermute | solution.py:12
  288.8 23.2 %collective-permute-start = (f32[2,16,64,128]{3,2,1,0:T(8,128)S(1)}, f32[2,16,64,128]{3,2,1,0:T(8,128)S(1)}, u32[]{:S(2)}, u32[]{:S(2)}) collective-permute-start(f32[2,16,64,128]{3,2,1,0:T(8,128)S(1)} %multiply_add_fusion.2), channel_id=1, source_target_pairs={{0,4},{4,8},{8,12},{12,16},{16,20},{20,24},{24,28},{1,5},{5,9},{9,... | collective-permute-start | bytes 3145736 | tf_op jit(solution)/shard_map/while/body/eval_jaxpr/ppermute | solution.py:12
  312.1 22.3 %collective-permute-start = (f32[2,16,64,128]{3,2,1,0:T(8,128)S(1)}, f32[2,16,64,128]{3,2,1,0:T(8,128)S(1)}, u32[]{:S(2)}, u32[]{:S(2)}) collective-permute-start(f32[2,16,64,128]{3,2,1,0:T(8,128)S(1)} %multiply_add_fusion.2), channel_id=1, source_target_pairs={{0,4},{4,8},{8,12},{12,16},{16,20},{20,24},{24,28},{1,5},{5,9},{9,... | collective-permute-start | bytes 3145736 | tf_op jit(solution)/shard_map/while/body/eval_jaxpr/ppermute | solution.py:12
  381.4 8.7 %copy-start.1 = (f32[2,1024]{1,0:T(2,128)S(1)}, f32[2,1024]{1,0:T(2,128)}, u32[]{:S(2)}) copy-start(f32[2,1024]{1,0:T(2,128)} %mul.139) | copy-start | bytes 24580
where the time goes:
time: 481 us; the launch traced here: 478 us
  waiting for transfers between devices  207 us (43%)
  local copies, waits for them, and re-layouts  106 us (22%)
  blocking collectives  51.9 us (11%)
  matrix products  41.3 us (9%)
  starting transfers between devices  39.8 us (8%)
  other arithmetic  31.6 us (7%)
    ppermute x7, waiting for transfers between devices, passed_along(): lax.ppermute(value, axis, [(source, source + steps) for source in range(l...  158 us
    all_to_all x1, blocking collectives, shards(): lax.all_to_all(mixed_here, 'head', split_axis=0, concat_axis=1, tiled=True)  51.9 us
    all_to_all x1, waiting for transfers between devices, shards(): lax.all_to_all(feature_groups, 'head', split_axis=1, concat_axis=0, tiled...  34.5 us
    convert_element_type x2, local copies, waits for them, and re-layouts, normalize(): values.astype(jnp.float32) * jax.nn.silu(gate_part.astype(jnp.float32))  24.5 us
    unnamed x12, local copies, waits for them, and re-layouts  18.8 us
    convert_element_type x2, local copies, waits for them, and re-layouts, normalize(): gate_part.astype(jnp.float32)  17.5 us
    ppermute x7, starting transfers between devices, passed_along(): lax.ppermute(value, axis, [(source, source + steps) for source in range(l...  15.5 us
    dot_general x2, matrix products, block_terms(): jnp.einsum('ghts,sghp->tghp', weights, feature_block, preferred_element_t...  14.7 us
  transfers between devices with their start and end apart: 13, of which 12 were waited for; matrix products, arithmetic and copies ran while one was open for 16% of the time, Pallas kernels for 0%

commit v1 on v0

--- a/solution.py
+++ b/solution.py
@@ -131,7 +131,12 @@
         local_groups, group_width
     )
     mixed_here = normalize(ssm_out, gate_here, gain_here)
-    restored = lax.all_to_all(mixed_here, "head", split_axis=0, concat_axis=1, tiled=True)
+    restored = jnp.concatenate(
+        lax.all_to_all(
+            jnp.stack(jnp.split(mixed_here, lax.axis_size("head"), axis=0)), "head", 0, 0
+        ),
+        axis=1,
+    )
     return restored.reshape(tok_rows, features.shape[1])
 
 

time: 481 us -> 459 us (0.954)
  local copies, waits for them, and re-layouts: 106 us -> 85.2 us
    convert_element_type x1 -> x0, local copies, waits for them, and re-layouts: 11.3 us -> none  [normalize(): return (gated_values * inverse_rms * gain_row).astype(jnp.bfloat16)]
    all_to_all x2 -> x0, local copies, waits for them, and re-layouts: 9.56 us -> none  [shards(): lax.all_to_all(mixed_here, 'head', split_axis=0, concat_axis=1, tiled=True)]
    another operation x3 -> x5, local copies, waits for them, and re-layouts: 0.12 us -> 6.71 us  [the longest x1 6.32 us: shards(): return restored.reshape(tok_rows, features.shape[1])]
    reshape x2 -> x1, local copies, waits for them, and re-layouts: 6.32 us -> 0.01 us  [the longest x1 6.31 us: shards(): return restored.reshape(tok_rows, features.shape[1])]
  transfers between devices with their start and end apart: 13 -> 13, of which waited for: 12 -> 12; matrix products, arithmetic and copies ran while one was open for 16% -> 17% of each run, Pallas kernels for 0% -> 0%
where the time goes in v1:
time: 459 us; the launch traced here: 456 us
  waiting for transfers between devices  207 us (45%)
  local copies, waits for them, and re-layouts  85.2 us (19%)
  blocking collectives  51.5 us (11%)
  matrix products  41.2 us (9%)
  starting transfers between devices  39.8 us (9%)
  other arithmetic  30.9 us (7%)
    ppermute x7, waiting for transfers between devices, passed_along(): lax.ppermute(value, axis, [(source, source + steps) for source in range(l...  158 us
    all_to_all x1, blocking collectives, shards(): lax.all_to_all(jnp.stack(jnp.split(mixed_here, lax.axis_size('head'), axi...  51.5 us
    all_to_all x1, waiting for transfers between devices, shards(): lax.all_to_all(feature_groups, 'head', split_axis=1, concat_axis=0, tiled...  34.4 us
    convert_element_type x2, local copies, waits for them, and re-layouts, normalize(): values.astype(jnp.float32) * jax.nn.silu(gate_part.astype(jnp.float32))  24.5 us
    unnamed x12, local copies, waits for them, and re-layouts  18.9 us
    convert_element_type x2, local copies, waits for them, and re-layouts, normalize(): gate_part.astype(jnp.float32)  17.4 us
    ppermute x7, starting transfers between devices, passed_along(): lax.ppermute(value, axis, [(source, source + steps) for source in range(l...  15.5 us
    dot_general x2, matrix products, block_terms(): jnp.einsum('ghts,sghp->tghp', weights, feature_block, preferred_element_t...  14.7 us
  transfers between devices with their start and end apart: 13, of which 12 were waited for; matrix products, arithmetic and copies ran while one was open for 17% of the time, Pallas kernels for 0%

profile of v1, /device:TPU:8, one launch (start us, length us, event | category | flops | bytes accessed | tf_op | source)
XLA Modules:
  0.0 456.1 jit_solution(14529890308424106190)
XLA Ops:
  21.6 6.4 %copy.114 = bf16[256,8192]{0,1:T(8,128)(2,1)} copy(bf16[256,8192]{1,0:T(8,128)(2,1)} %param.14) | data formatting | bytes 8388608 | tf_op args[0]
  28.0 6.5 %copy.115 = bf16[256,8,1024]{2,0,1:T(8,128)(2,1)} copy(bf16[256,8,1024]{0,2,1:T(8,128)(2,1)} %bitcast.170) | data formatting | bytes 8388608 | tf_op jit(solution)/shard_map/reshape | solution.py:57
  34.5 5.0 %all-to-all-start = ((bf16[256,8,1024]{2,0,1:T(8,128)(2,1)}), bf16[256,8,1024]{2,0,1:T(8,128)(2,1)}, u32[]{:S(2)}, u32[]{:S(2)}) async-start(bf16[256,8,1024]{2,0,1:T(8,128)(2,1)} %copy.115), calls=%async_computation | async-start | bytes 8388608 | tf_op jit(solution)/shard_map/all_to_all | solution.py:62
  40.5 6.4 %copy.128 = bf16[256,8192]{0,1:T(8,128)(2,1)} copy(bf16[256,8192]{1,0:T(8,128)(2,1)} %param.15) | data formatting | bytes 8388608 | tf_op args[1]
  48.2 4.6 reduce-window.6
  53.3 34.4 %all-to-all-done = bf16[256,8,1024]{2,0,1:T(8,128)(2,1)} async-done(((bf16[256,8,1024]{2,0,1:T(8,128)(2,1)}), bf16[256,8,1024]{2,0,1:T(8,128)(2,1)}, u32[]{:S(2)}, u32[]{:S(2)}) %all-to-all-start) | async-done | bytes 4194336 | tf_op jit(solution)/shard_map/all_to_all | solution.py:62
  91.5 6.3 %copy.116 = bf16[256,4,2,1024]{0,3,2,1:T(8,128)(2,1)} copy(bf16[256,4,2,1024]{3,0,2,1:T(8,128)(2,1)} %bitcast.13) | data formatting | bytes 8388608 | tf_op jit(solution)/shard_map/all_to_all | solution.py:62
  100.0 5.0 %all-to-all-start.5 = ((bf16[256,8,1024]{0,2,1:T(8,128)(2,1)}), bf16[256,8,1024]{0,2,1:T(8,128)(2,1)}, u32[]{:S(2)}, u32[]{:S(2)}) async-start(bf16[256,8,1024]{0,2,1:T(8,128)(2,1)} %bitcast.168), calls=%async_computation.5 | async-start | bytes 8388608 | tf_op jit(solution)/shard_map/all_to_all | solution.py:63
  105.0 31.4 %while.35 = (s32[]{:T(128)}, f32[2,2,256,2,16,64]{2,5,4,3,1,0:T(8,128)}, f32[2,2,2,16,64,128]{5,4,3,2,1,0:T(8,128)}, bf16[2,2,256,2,16,64]{2,5,4,3,1,0:T(8,128)(...) while((s32[]{:T(128)}, ...), condition=%wide.region_3.4_spmd, body=%wide.region_2.3_spmd.sunk | while | flops 902004736 | bytes 15929189 | solution.py:84
  107.6 7.3 %bitcast_dynamic-update-slice_fusion.6 = f32[2,2,256,2,16,64]{2,5,4,3,1,0:T(8,128)} fusion(f32[2,2,256,2,16,64]{2,5,4,3,1,0:T(8,128)} %get-tuple-element.332, s32[]{:T(128)} %get-tuple-element.331, f32[2,2,16,256]{3,2,1,0:T(8,128)S(1)} %copy.155, f32[2,2,16,256]{3,2,1,0:T(8,128)S(1)} %copy.157, f32[2,2,256,256]{3,2,1,0:T(8,128)S(1)} %fusion.52, ...), kind=kOutput, calls=%fused_computation.10.clone.1 | convolution fusion | flops 562036736 | bytes 7603200 | tf_op jit(solution)/shard_map/while/body/eval_jaxpr/vmap(ghts,sghp->tghp)/dot_general | solution.py:26
  115.6 5.1 %bitcast_dynamic-update-slice_fusion.7 = f32[2,2,2,16,64,128]{5,4,3,2,1,0:T(8,128)} fusion(f32[2,2,2,16,64,128]{5,4,3,2,1,0:T(8,128)} %get-tuple-element.333, s32[]{:T(128)} %get-tuple-element.331, f32[2,256,2,16]{1,3,2,0:T(8,128)S(1)} %copy.158, f32[2,256,2,128]{3,1,2,0:T(8,128)S(1)} %bitcast_convert_fusion.2, ...), kind=kOutput, calls=%fused_computation.13.clone.1 | convolution fusion | flops 272629760 | bytes 4785152 | tf_op jit(solution)/shard_map/while/body/eval_jaxpr/vmap(sghn,sghp->ghpn)/dot_general | solution.py:33
  123.3 7.3 %bitcast_dynamic-update-slice_fusion.6 = f32[2,2,256,2,16,64]{2,5,4,3,1,0:T(8,128)} fusion(f32[2,2,256,2,16,64]{2,5,4,3,1,0:T(8,128)} %get-tuple-element.332, s32[]{:T(128)} %get-tuple-element.331, f32[2,2,16,256]{3,2,1,0:T(8,128)S(1)} %copy.155, f32[2,2,16,256]{3,2,1,0:T(8,128)S(1)} %copy.157, f32[2,2,256,256]{3,2,1,0:T(8,128)S(1)} %fusion.52, ...), kind=kOutput, calls=%fused_computation.10.clone.1 | convolution fusion | flops 562036736 | bytes 7603200 | tf_op jit(solution)/shard_map/while/body/eval_jaxpr/vmap(ghts,sghp->tghp)/dot_general | solution.py:26
  131.3 5.1 %bitcast_dynamic-update-slice_fusion.7 = f32[2,2,2,16,64,128]{5,4,3,2,1,0:T(8,128)} fusion(f32[2,2,2,16,64,128]{5,4,3,2,1,0:T(8,128)} %get-tuple-element.333, s32[]{:T(128)} %get-tuple-element.331, f32[2,256,2,16]{1,3,2,0:T(8,128)S(1)} %copy.158, f32[2,256,2,128]{3,1,2,0:T(8,128)S(1)} %bitcast_convert_fusion.2, ...), kind=kOutput, calls=%fused_computation.13.clone.1 | convolution fusion | flops 272629760 | bytes 4785152 | tf_op jit(solution)/shard_map/while/body/eval_jaxpr/vmap(sghn,sghp->ghpn)/dot_general | solution.py:33
  136.4 10.0 %while.37 = (s32[]{:T(128)}, f32[2,16,64,128]{3,2,1,0:T(8,128)S(1)}, f32[4,2,16,64,128]{4,3,2,1,0:T(8,128)}, f32[4,2,16]{2,1,0:T(2,128)S(1)}, f32[4,2,16,64,128]{4,3,2,1,0:T(8,128)}, /*index=5*/s32[]{:T(128)}, s32[]{:T(128)}) while((s32[]{:T(128)}, f32[2,16,64,128]{3,2,1,0:T(8,128)S(1)}, f32[4,2,16,64,128]{4,3,2,1,0:T(8,128)}, ...), condition=%wide.region_5.6_spmd.clone, body=%wide.region_4.5_spmd.clone.sunk | while | flops 1048579 | bytes 5243872 | solution.py:103
  146.5 6.6 %all-to-all-done.5 = bf16[256,8,1024]{0,2,1:T(8,128)(2,1)} async-done(((bf16[256,8,1024]{0,2,1:T(8,128)(2,1)}), bf16[256,8,1024]{0,2,1:T(8,128)(2,1)}, u32[]{:S(2)}, u32[]{:S(2)}) %all-to-all-start.5) | async-done | bytes 4194336 | tf_op jit(solution)/shard_map/all_to_all | solution.py:63
  153.0 6.2 %convert_element_type.75 = f32[256,8,1024]{0,2,1:T(8,128)} convert(bf16[256,8,1024]{0,2,1:T(8,128)(2,1)} %all-to-all-done.5) | non-fusion elementwise | flops 2097152 | bytes 12582912 | tf_op jit(solution)/shard_map/convert_element_type | solution.py:40
  159.3 175.0 %while.36 = (s32[]{:T(128)}, f32[2,16,64,128]{3,2,1,0:T(8,128)S(1)}, f32[2,16]{1,0:T(2,128)S(1)}, f32[2,16,64,128]{3,2,1,0:T(8,128)S(1)}, s32[]{:T(128)}) while((s32[]{:T(128)}, f32[2,16,64,128]{3,2,1,0:T(8,128)S(1)}, f32[2,16]{1,0:T(2,128)S(1)}, f32[2,16,64,128]{3,2,1,0:T(8,128)S(1)}, s32[]{:T(128)}) %tuple.68), condition=%wide.region_10.11_spmd, body=%wide.region_9.10_spmd.sunk | while | flops 524290 | bytes 7340261 | solution.py:111
  162.9 24.0 %collective-permute-done = f32[2,16,64,128]{3,2,1,0:T(8,128)S(1)} collective-permute-done((f32[2,16,64,128]{3,2,1,0:T(8,128)S(1)}, f32[2,16,64,128]{3,2,1,0:T(8,128)S(1)}, u32[]{:S(2)}, u32[]{:S(2)}) %collective-permute-start) | collective-permute-done | bytes 1048608 | tf_op jit(solution)/shard_map/while/body/eval_jaxpr/ppermute | solution.py:12
  189.6 24.0 %collective-permute-done = f32[2,16,64,128]{3,2,1,0:T(8,128)S(1)} collective-permute-done((f32[2,16,64,128]{3,2,1,0:T(8,128)S(1)}, f32[2,16,64,128]{3,2,1,0:T(8,128)S(1)}, u32[]{:S(2)}, u32[]{:S(2)}) %collective-permute-start) | collective-permute-done | bytes 1048608 | tf_op jit(solution)/shard_map/while/body/eval_jaxpr/ppermute | solution.py:12
  215.7 23.8 %collective-permute-done = f32[2,16,64,128]{3,2,1,0:T(8,128)S(1)} collective-permute-done((f32[2,16,64,128]{3,2,1,0:T(8,128)S(1)}, f32[2,16,64,128]{3,2,1,0:T(8,128)S(1)}, u32[]{:S(2)}, u32[]{:S(2)}) %collective-permute-start) | collective-permute-done | bytes 1048608 | tf_op jit(solution)/shard_map/while/body/eval_jaxpr/ppermute | solution.py:12
  241.6 22.9 %collective-permute-done = f32[2,16,64,128]{3,2,1,0:T(8,128)S(1)} collective-permute-done((f32[2,16,64,128]{3,2,1,0:T(8,128)S(1)}, f32[2,16,64,128]{3,2,1,0:T(8,128)S(1)}, u32[]{:S(2)}, u32[]{:S(2)}) %collective-permute-start) | collective-permute-done | bytes 1048608 | tf_op jit(solution)/shard_map/while/body/eval_jaxpr/ppermute | solution.py:12
  266.6 22.0 %collective-permute-done = f32[2,16,64,128]{3,2,1,0:T(8,128)S(1)} collective-permute-done((f32[2,16,64,128]{3,2,1,0:T(8,128)S(1)}, f32[2,16,64,128]{3,2,1,0:T(8,128)S(1)}, u32[]{:S(2)}, u32[]{:S(2)}) %collective-permute-start) | collective-permute-done | bytes 1048608 | tf_op jit(solution)/shard_map/while/body/eval_jaxpr/ppermute | solution.py:12
  290.7 21.2 %collective-permute-done = f32[2,16,64,128]{3,2,1,0:T(8,128)S(1)} collective-permute-done((f32[2,16,64,128]{3,2,1,0:T(8,128)S(1)}, f32[2,16,64,128]{3,2,1,0:T(8,128)S(1)}, u32[]{:S(2)}, u32[]{:S(2)}) %collective-permute-start) | collective-permute-done | bytes 1048608 | tf_op jit(solution)/shard_map/while/body/eval_jaxpr/ppermute | solution.py:12
  314.0 20.3 %collective-permute-done = f32[2,16,64,128]{3,2,1,0:T(8,128)S(1)} collective-permute-done((f32[2,16,64,128]{3,2,1,0:T(8,128)S(1)}, f32[2,16,64,128]{3,2,1,0:T(8,128)S(1)}, u32[]{:S(2)}, u32[]{:S(2)}) %collective-permute-start) | collective-permute-done | bytes 1048608 | tf_op jit(solution)/shard_map/while/body/eval_jaxpr/ppermute | solution.py:12
  334.4 13.8 %multiply_reduce_fusion = (f32[4,256,2]{1,2,0:T(2,128)S(1)}, f32[4,256,2,16,64]{1,4,3,2,0:T(8,128)}) fusion(f32[4,256,2,16,64]{1,4,3,2,0:T(8,128)} %bitcast.164, bf16[4,256,2,16,64]{1,4,3,2,0:T(8,128)(2,1)} %bitcast.173, f32[2,16]{1,0:T(2,128)S(1)} %mul.128, f32[4,256,2,16]{1,3,2,0:T(8,128)S(1)} %bitcast_exponential_fusion, ...), kind=kOutput, calls=%fused_computation.43 | convolution fusion | flops 3252680704 | bytes 35267200 | tf_op jit(solution)/shard_map/ktgn,kghpn->ktghp/dot_general | solution.py:114
  348.1 13.8 %copy.127 = f32[4,256,2,16,64]{1,0,4,3,2:T(4,128)} copy(f32[4,256,2,16,64]{1,4,3,2,0:T(8,128)} %get-tuple-element.212) | data formatting | bytes 16777216 | tf_op jit(solution)/shard_map/convert_element_type | solution.py:40
  361.9 10.7 %reshape.130 = f32[1024,2,1024]{0,2,1:T(8,128)} reshape(f32[4,256,2,16,64]{1,0,4,3,2:T(4,128)} %copy.127) | data formatting | bytes 16777216 | tf_op jit(solution)/shard_map/convert_element_type | solution.py:40
  372.7 8.7 %copy.130 = f32[4,256,2,1024]{3,1,0,2:T(8,128)} copy(f32[4,256,2,1024]{1,3,2,0:T(8,128)} %bitcast.165) | data formatting | bytes 16777216 | tf_op jit(solution)/shard_map/convert_element_type | solution.py:40
  381.4 8.7 %copy.132 = f32[1024,2,1024]{0,2,1:T(8,128)} copy(f32[1024,2,1024]{2,0,1:T(8,128)} %bitcast.166) | data formatting | bytes 16777216 | tf_op jit(solution)/shard_map/convert_element_type | solution.py:40
  390.1 7.3 %multiply_convert_fusion.4 = bf16[1024,2,1024]{0,2,1:T(8,128)(2,1)S(1)} fusion(f32[1024,2,1024]{0,2,1:T(8,128)} %reshape.130, f32[1024,2,1024]{0,2,1:T(8,128)} %copy.132, f32[2,1024]{1,0:T(2,128)S(1)} %copy-done.1, f32[1024,2]{0,1:T(2,128)S(1)} %bitcast.180), kind=kLoop, calls=%fused_computation.42 | loop fusion | flops 16777216 | bytes 20987904 | tf_op jit(solution)/shard_map/convert_element_type | solution.py:42
  398.3 51.5 %all_to_all.86 = bf16[4,256,2,1024]{1,3,2,0:T(8,128)(2,1)} all-to-all(bf16[4,256,2,1024]{1,3,2,0:T(8,128)(2,1)S(1)} %pad_maximum_fusion), channel_id=1, replica_groups=mesh['seq'=8,'head'=4] {'head'}, dimensions={0} | all-to-all | bytes 8388608 | tf_op jit(solution)/shard_map/all_to_all | solution.py:135
  449.8 6.3 %copy.134 = bf16[256,8192]{1,0:T(8,128)(2,1)} copy(bf16[256,8192]{0,1:T(8,128)(2,1)} %bitcast.169) | data formatting | bytes 8388608 | tf_op jit(solution)/shard_map/reshape;reshape | solution.py:140
  (90 shorter events, 64.2 us)
Async XLA Ops:
  1.7 7.9 %all-to-all-start.3 = ((f32[256,8,16]{0,2,1:T(8,128)}), f32[256,8,16]{0,2,1:T(8,128)S(1)}, u32[]{:S(2)}, u32[]{:S(2)}) async-start(f32[256,8,16]{0,2,1:T(8,128)} %bitcast.22), calls=%async_computation.3 | async-start | bytes 262144 | tf_op jit(solution)/shard_map/all_to_all | solution.py:69
  9.6 7.9 %all-to-all-start.4 = ((f32[256,8,16]{0,2,1:T(8,128)}), f32[256,8,16]{0,2,1:T(8,128)S(1)}, u32[]{:S(2)}, u32[]{:S(2)}) async-start(f32[256,8,16]{0,2,1:T(8,128)} %bitcast.28), calls=%async_computation.4 | async-start | bytes 262144 | tf_op jit(solution)/shard_map/all_to_all | solution.py:68
  17.5 17.1 %all-to-all-start.1 = ((bf16[256,8,128]{2,0,1:T(8,128)(2,1)}), bf16[256,8,128]{2,0,1:T(8,128)(2,1)}, u32[]{:S(2)}, u32[]{:S(2)}) async-start(bf16[256,8,128]{2,0,1:T(8,128)(2,1)} %copy.117), calls=%async_computation.1 | async-start | bytes 1048576 | tf_op jit(solution)/shard_map/all_to_all | solution.py:65
  28.0 11.6 %copy-start = (bf16[256,8,128]{2,1,0:T(8,128)(2,1)S(1)}, bf16[256,8,128]{2,1,0:T(8,128)(2,1)}, u32[]{:S(2)}) copy-start(bf16[256,8,128]{2,1,0:T(8,128)(2,1)} %param.16) | copy-start | bytes 1572868
  34.5 12.3 %copy-start.2 = (f32[32]{0:T(128)S(1)}, f32[32]{0:T(128)}, u32[]{:S(2)}) copy-start(f32[32]{0:T(128)} %param.20) | copy-start | bytes 388
  34.5 53.2 %all-to-all-start = ((bf16[256,8,1024]{2,0,1:T(8,128)(2,1)}), bf16[256,8,1024]{2,0,1:T(8,128)(2,1)}, u32[]{:S(2)}, u32[]{:S(2)}) async-start(bf16[256,8,1024]{2,0,1:T(8,128)(2,1)} %copy.115), calls=%async_computation | async-start | bytes 8388608 | tf_op jit(solution)/shard_map/all_to_all | solution.py:62
  87.7 12.3 %all-to-all-start.2 = ((bf16[256,8,128]{2,0,1:T(8,128)(2,1)}), bf16[256,8,128]{2,0,1:T(8,128)(2,1)S(1)}, u32[]{:S(2)}, u32[]{:S(2)}) async-start(bf16[256,8,128]{2,0,1:T(8,128)(2,1)} %copy.118), calls=%async_computation.2 | async-start | bytes 1048576 | tf_op jit(solution)/shard_map/all_to_all | solution.py:64
  100.0 53.1 %all-to-all-start.5 = ((bf16[256,8,1024]{0,2,1:T(8,128)(2,1)}), bf16[256,8,1024]{0,2,1:T(8,128)(2,1)}, u32[]{:S(2)}, u32[]{:S(2)}) async-start(bf16[256,8,1024]{0,2,1:T(8,128)(2,1)} %bitcast.168), calls=%async_computation.5 | async-start | bytes 8388608 | tf_op jit(solution)/shard_map/all_to_all | solution.py:63
  159.5 27.4 %collective-permute-start = (f32[2,16,64,128]{3,2,1,0:T(8,128)S(1)}, f32[2,16,64,128]{3,2,1,0:T(8,128)S(1)}, u32[]{:S(2)}, u32[]{:S(2)}) collective-permute-start(f32[2,16,64,128]{3,2,1,0:T(8,128)S(1)} %multiply_add_fusion.2), channel_id=1, source_target_pairs={{0,4},{4,8},{8,12},{12,16},{16,20},{20,24},{24,28},{1,5},{5,9},{9,... | collective-permute-start | bytes 3145736 | tf_op jit(solution)/shard_map/while/body/eval_jaxpr/ppermute | solution.py:12
  187.1 26.5 %collective-permute-start = (f32[2,16,64,128]{3,2,1,0:T(8,128)S(1)}, f32[2,16,64,128]{3,2,1,0:T(8,128)S(1)}, u32[]{:S(2)}, u32[]{:S(2)}) collective-permute-start(f32[2,16,64,128]{3,2,1,0:T(8,128)S(1)} %multiply_add_fusion.2), channel_id=1, source_target_pairs={{0,4},{4,8},{8,12},{12,16},{16,20},{20,24},{24,28},{1,5},{5,9},{9,... | collective-permute-start | bytes 3145736 | tf_op jit(solution)/shard_map/while/body/eval_jaxpr/ppermute | solution.py:12
  213.8 25.7 %collective-permute-start = (f32[2,16,64,128]{3,2,1,0:T(8,128)S(1)}, f32[2,16,64,128]{3,2,1,0:T(8,128)S(1)}, u32[]{:S(2)}, u32[]{:S(2)}) collective-permute-start(f32[2,16,64,128]{3,2,1,0:T(8,128)S(1)} %multiply_add_fusion.2), channel_id=1, source_target_pairs={{0,4},{4,8},{8,12},{12,16},{16,20},{20,24},{24,28},{1,5},{5,9},{9,... | collective-permute-start | bytes 3145736 | tf_op jit(solution)/shard_map/while/body/eval_jaxpr/ppermute | solution.py:12
  239.6 24.8 %collective-permute-start = (f32[2,16,64,128]{3,2,1,0:T(8,128)S(1)}, f32[2,16,64,128]{3,2,1,0:T(8,128)S(1)}, u32[]{:S(2)}, u32[]{:S(2)}) collective-permute-start(f32[2,16,64,128]{3,2,1,0:T(8,128)S(1)} %multiply_add_fusion.2), channel_id=1, source_target_pairs={{0,4},{4,8},{8,12},{12,16},{16,20},{20,24},{24,28},{1,5},{5,9},{9,... | collective-permute-start | bytes 3145736 | tf_op jit(solution)/shard_map/while/body/eval_jaxpr/ppermute | solution.py:12
  264.6 24.0 %collective-permute-start = (f32[2,16,64,128]{3,2,1,0:T(8,128)S(1)}, f32[2,16,64,128]{3,2,1,0:T(8,128)S(1)}, u32[]{:S(2)}, u32[]{:S(2)}) collective-permute-start(f32[2,16,64,128]{3,2,1,0:T(8,128)S(1)} %multiply_add_fusion.2), channel_id=1, source_target_pairs={{0,4},{4,8},{8,12},{12,16},{16,20},{20,24},{24,28},{1,5},{5,9},{9,... | collective-permute-start | bytes 3145736 | tf_op jit(solution)/shard_map/while/body/eval_jaxpr/ppermute | solution.py:12
  288.8 23.2 %collective-permute-start = (f32[2,16,64,128]{3,2,1,0:T(8,128)S(1)}, f32[2,16,64,128]{3,2,1,0:T(8,128)S(1)}, u32[]{:S(2)}, u32[]{:S(2)}) collective-permute-start(f32[2,16,64,128]{3,2,1,0:T(8,128)S(1)} %multiply_add_fusion.2), channel_id=1, source_target_pairs={{0,4},{4,8},{8,12},{12,16},{16,20},{20,24},{24,28},{1,5},{5,9},{9,... | collective-permute-start | bytes 3145736 | tf_op jit(solution)/shard_map/while/body/eval_jaxpr/ppermute | solution.py:12
  312.1 22.3 %collective-permute-start = (f32[2,16,64,128]{3,2,1,0:T(8,128)S(1)}, f32[2,16,64,128]{3,2,1,0:T(8,128)S(1)}, u32[]{:S(2)}, u32[]{:S(2)}) collective-permute-start(f32[2,16,64,128]{3,2,1,0:T(8,128)S(1)} %multiply_add_fusion.2), channel_id=1, source_target_pairs={{0,4},{4,8},{8,12},{12,16},{16,20},{20,24},{24,28},{1,5},{5,9},{9,... | collective-permute-start | bytes 3145736 | tf_op jit(solution)/shard_map/while/body/eval_jaxpr/ppermute | solution.py:12
  381.4 8.7 %copy-start.1 = (f32[2,1024]{1,0:T(2,128)S(1)}, f32[2,1024]{1,0:T(2,128)}, u32[]{:S(2)}) copy-start(f32[2,1024]{1,0:T(2,128)} %mul.139) | copy-start | bytes 24580
